TPU v7x, 32 devices: a whole 2x2x4 slice. The times are simulated.
32 devices in a mesh: groups: 2 (over y), frame: 16 (over z, x, core).
Axes of the slice: x: 2, y: 2, z: 4, core: 2. Of those that a mesh axis runs over, the one named last changes fastest.
Arguments:
- queries: bfloat16 [8192, 1536], P(('groups', 'frame')), parts along dimension 0, may hold values from -14 to 14
- key_heads: bfloat16 [8192, 1536], P(('groups', 'frame')), parts along dimension 0, may hold values from -14 to 14
- value_heads: bfloat16 [8192, 1536], P(('groups', 'frame')), parts along dimension 0, may hold values from -6 to 6
- tile_lists: int32 [16, 8], P('frame'), may hold values from 0 to 1
Outputs:
- attended: bfloat16 [8192, 1536], P(('groups', 'frame')), parts along dimension 0
There are 2 independent parts, one for each index of `groups`. A program takes and returns all parts, laid end to end along the dimension named above; an argument that names none is the same for every part. Nothing has to cross between parts.
Inputs may be any that keep to these rules, and one draw needn't show every extreme that they name: `tile_lists`: entry l of a frame's row names a block of the frame 2^l before it, entry 4 + l one of the frame 2^l after it; entries for frames outside the video are not read.
All inputs are finite; a program needn't handle non-finite values.
Results may differ from a plain program's by a relative error of at most 0.0049.
Values may be sent and summed in bfloat16 or wider, within the bound.
A program may use at most 64 MiB of HBM per device.

v0:
```python
import functools
import math

import jax
import jax.numpy as jnp
from jax import lax
from jax.experimental import pallas as pl
from jax.experimental.pallas import tpu as pltpu
from jax.sharding import PartitionSpec as P

HD = 128
TILE = 128
CHUNKS = 2
MESH = pl.DeviceIdType.MESH

CORE, ACROSS, ACROSS_RELAYED, MIRROR, BELOW8, ABOVE8 = range(6)
NEAR = 6


def kernel(n, levels, heads, *refs):
    q_ref, k_ref, v_ref, own_list, list_ref, out_ref = refs[:6]
    w_low = refs[6 : 6 + CHUNKS]
    w_high = refs[6 + CHUNKS : 6 + 2 * CHUNKS]
    (stage, landed, lists_v, lists_s, top, total, acc,
     w_send, w_recv, t_send, t_recv, l_send, l_recv, s_sem) = refs[6 + 2 * CHUNKS :]
    me = lax.axis_index("frame")
    quarter = me % 4
    x = quarter // 2
    core = me % 2
    core_peer = me + 1 - 2 * core
    across = me + 2 - 4 * x
    mirror = me + 3 - 2 * quarter
    has_low, has_high = me >= 4, me + 4 < n
    per = heads // CHUNKS
    width = per * HD
    far = [1 << level for level in range(4, levels)]
    yes = me >= 0

    partners = [
        (core_peer, yes, 0, 0),
        (across, yes, 1, 1),
        (mirror, yes, 2, 2),
        (me - 4, has_low, 3, 4),
        (me + 4, has_high, 4, 3),
    ]
    for j, d in enumerate(far):
        partners.append((me - d, me >= d, 5 + 2 * j, 6 + 2 * j))
        partners.append((me + d, me + d < n, 6 + 2 * j, 5 + 2 * j))

    barrier = pltpu.get_barrier_semaphore()
    for device, exists, _, _ in partners:
        @pl.when(exists)
        def _():
            pl.semaphore_signal(barrier, inc=1, device_id={"frame": device}, device_id_type=MESH)
    pl.semaphore_wait(barrier, sum(jnp.where(exists, 1, 0) for _, exists, _, _ in partners))

    def list_copy(device, here, there):
        return pltpu.make_async_remote_copy(
            src_ref=list_ref, dst_ref=lists_v.at[there],
            send_sem=l_send.at[here], recv_sem=l_recv.at[there],
            device_id={"frame": device}, device_id_type=MESH)

    def list_wait(here):
        return pltpu.make_async_remote_copy(
            src_ref=list_ref, dst_ref=lists_v.at[here],
            send_sem=l_send.at[here], recv_sem=l_recv.at[here],
            device_id={"frame": core_peer}, device_id_type=MESH)

    for device, exists, here, there in partners:
        @pl.when(exists)
        def _():
            list_copy(device, here, there).start()

    def whole_copy(side, chunk, kv):
        source = (k_ref, v_ref)[kv]
        target = (w_low, w_high)[side][chunk]
        return pltpu.make_async_remote_copy(
            src_ref=source.at[:, :, pl.ds(chunk * width, width)], dst_ref=target.at[kv],
            send_sem=w_send.at[side, chunk, kv], recv_sem=w_recv.at[side, chunk, kv],
            device_id={"frame": me + 4 if side == 0 else me - 4}, device_id_type=MESH)

    sides = ((has_high, has_low), (has_low, has_high))
    for chunk in range(CHUNKS):
        for side in range(2):
            @pl.when(sides[side][0])
            def _():
                for kv in range(2):
                    whole_copy(side, chunk, kv).start()

    for _, exists, here, _ in partners:
        @pl.when(exists)
        def _():
            list_wait(here).wait_recv()
            pltpu.make_async_copy(lists_v.at[here], lists_s.at[here], s_sem.at[here]).start()
    for _, exists, here, _ in partners:
        @pl.when(exists)
        def _():
            pltpu.make_async_copy(lists_v.at[here], lists_s.at[here], s_sem.at[here]).wait()

    def tile_copy(slot, chunk, device):
        return pltpu.make_async_remote_copy(
            src_ref=stage.at[slot, chunk], dst_ref=landed.at[slot, chunk],
            send_sem=t_send.at[slot, chunk], recv_sem=t_recv.at[slot, chunk],
            device_id={"frame": device}, device_id_type=MESH)

    def stage_own(slot, chunk, wanted):
        stage[slot, chunk, 0] = k_ref[wanted, :, pl.ds(chunk * width, width)]
        stage[slot, chunk, 1] = v_ref[wanted, :, pl.ds(chunk * width, width)]

    def stage_whole(slot, chunk, whole, wanted):
        stage[slot, chunk, 0] = whole[chunk][0, wanted]
        stage[slot, chunk, 1] = whole[chunk][1, wanted]

    inner = (quarter == 1) | (quarter == 2)
    far_sends = []
    for j, d in enumerate(far):
        far_sends.append((NEAR + 2 * j, me + d, me + d < n, 6 + 2 * j, 4 + j))
        far_sends.append((NEAR + 2 * j + 1, me - d, me >= d, 5 + 2 * j, levels + 4 + j))

    for chunk in range(CHUNKS):
        stage_own(ACROSS, chunk, lists_s[1, 0, 1 + levels * x])
        stage_own(CORE, chunk, lists_s[0, 0, levels * core])
        @pl.when(inner)
        def _():
            stage_own(MIRROR, chunk, lists_s[2, 0, levels * (x)])
        for slot, _, exists, here, entry in far_sends:
            @pl.when(exists)
            def _():
                stage_own(slot, chunk, lists_s[here, 0, entry])
    for chunk in range(CHUNKS):
        tile_copy(CORE, chunk, core_peer).start()
        @pl.when(inner)
        def _():
            tile_copy(MIRROR, chunk, mirror).start()
        tile_copy(ACROSS, chunk, across).start()
        for slot, device, exists, _, _ in far_sends:
            @pl.when(exists)
            def _():
                tile_copy(slot, chunk, device).start()

    factor = math.log2(math.e) / math.sqrt(HD)

    def one_head(h, keys, values, first):
        columns = pl.ds(pl.multiple_of(h * HD, HD), HD)
        scores = lax.dot_general(
            q_ref[:, columns], keys, (((1,), (1,)), ((), ())), preferred_element_type=jnp.float32)
        peak = jnp.max(scores, axis=1, keepdims=True)
        if not first:
            old = top[h][:, :1]
            peak = jnp.maximum(old, peak)
        raised = jnp.exp2((scores - peak) * factor)
        added = jnp.sum(raised, axis=1, keepdims=True)
        mixed = jnp.dot(raised.astype(jnp.bfloat16), values, preferred_element_type=jnp.float32)
        if not first:
            fade = jnp.exp2((old - peak) * factor)
            added = added + fade * total[h][:, :1]
            mixed = mixed + fade * acc[h]
        top[h] = jnp.broadcast_to(peak, (peak.shape[0], HD))
        total[h] = jnp.broadcast_to(added, (peak.shape[0], HD))
        acc[h] = mixed

    def attend(chunk, load, first=False):
        def step(i, carry):
            for j in range(2):
                local = i * 2 + j
                keys, values = load(pl.ds(pl.multiple_of(local * HD, HD), HD))
                one_head(chunk * per + local, keys, values, first)
            return carry
        lax.fori_loop(0, per // 2, step, 0)

    def attend_own(chunk):
        def load(columns):
            columns = pl.ds(pl.multiple_of(columns.start + chunk * width, HD), HD)
            keys, values = k_ref[:, :, columns], v_ref[:, :, columns]
            return keys.reshape(-1, HD), values.reshape(-1, HD)
        attend(chunk, load, True)

    def attend_whole(side, chunk):
        wanted = own_list[0, 2 + levels * side]
        whole = (w_low, w_high)[side][chunk]
        attend(chunk, lambda columns: (whole[0, wanted, :, columns], whole[1, wanted, :, columns]))

    def attend_landed(slot, chunk, exists):
        @pl.when(exists)
        def _():
            tile_copy(slot, chunk, core_peer).wait_recv()
            attend(chunk, lambda columns: (landed[slot, chunk, 0, :, columns], landed[slot, chunk, 1, :, columns]))

    def wait_whole(chunk):
        for side in range(2):
            @pl.when(sides[side][1])
            def _():
                for kv in range(2):
                    whole_copy(side, chunk, kv).wait_recv()

    relays = [
        (ACROSS_RELAYED, across, (x == 0) & has_high, w_high, 1, levels + 1),
        (ACROSS_RELAYED, across, (x == 1) & has_low, w_low, 1, 1),
        (MIRROR, mirror, (quarter == 0) & has_high, w_high, 2, levels),
        (MIRROR, mirror, (quarter == 3) & has_low, w_low, 2, 0),
        (BELOW8, me + 4, has_low & has_high, w_low, 4, 3),
        (ABOVE8, me - 4, has_low & has_high, w_high, 3, levels + 3),
    ]

    def relay(chunk):
        for slot, _, exists, whole, here, entry in relays:
            @pl.when(exists)
            def _():
                stage_whole(slot, chunk, whole, lists_s[here, 0, entry])
        for slot, device, exists, _, _, _ in relays:
            @pl.when(exists)
            def _():
                tile_copy(slot, chunk, device).start()

    def attend_wholes(chunk):
        for side in range(2):
            @pl.when(sides[side][1])
            def _():
                attend_whole(side, chunk)

    relayed_across = ((x == 0) & has_low) | ((x == 1) & has_high)
    outer = ((quarter == 0) & has_low) | ((quarter == 3) & has_high)

    for chunk in range(CHUNKS):
        attend_own(chunk)
    for chunk in range(CHUNKS):
        wait_whole(chunk)
        relay(chunk)
        attend_landed(CORE, chunk, yes)
        attend_wholes(chunk)
        attend_landed(ACROSS, chunk, yes)
    for chunk in range(CHUNKS):
        for j, d in enumerate(far):
            attend_landed(NEAR + 2 * j, chunk, me >= d)
            attend_landed(NEAR + 2 * j + 1, chunk, me + d < n)
        attend_landed(MIRROR, chunk, inner | outer)
        attend_landed(BELOW8, chunk, me >= 8)
        attend_landed(ABOVE8, chunk, me + 8 < n)
        attend_landed(ACROSS_RELAYED, chunk, relayed_across)
        for local in range(per):
            h = chunk * per + local
            out_ref[:, pl.ds(h * HD, HD)] = (acc[h] / total[h]).astype(out_ref.dtype)

    for _, exists, here, _ in partners:
        @pl.when(exists)
        def _():
            list_wait(here).wait_send()
    for chunk in range(CHUNKS):
        for side in range(2):
            @pl.when(sides[side][0])
            def _():
                for kv in range(2):
                    whole_copy(side, chunk, kv).wait_send()
        sent = [(CORE, yes), (ACROSS, yes), (MIRROR, inner)]
        sent += [(slot, exists) for slot, _, exists, _, _ in far_sends]
        sent += [(slot, exists) for slot, _, exists, _, _, _ in relays]
        for slot, exists in sent:
            @pl.when(exists)
            def _():
                tile_copy(slot, chunk, core_peer).wait_send()


def solution(mesh):
    n = mesh.shape["frame"]

    def body(queries, key_heads, value_heads, tile_lists):
        rows, channels = queries.shape
        heads = channels // HD
        tiles = rows // TILE
        levels = tile_lists.shape[1] // 2
        far = max(levels - 4, 0)
        width = channels // CHUNKS
        slots = NEAR + 2 * far
        lists = 5 + 2 * far
        padded = jnp.pad(tile_lists, ((0, 7), (0, 128 - 2 * levels)))
        vmem = pl.BlockSpec(memory_space=pltpu.VMEM)
        dma = pltpu.SemaphoreType.DMA
        whole = pltpu.VMEM((2, tiles, TILE, width), jnp.bfloat16)
        return pl.pallas_call(
            functools.partial(kernel, n, levels, heads),
            out_shape=jax.ShapeDtypeStruct((rows, channels), jnp.bfloat16),
            in_specs=[vmem, vmem, vmem, pl.BlockSpec(memory_space=pltpu.SMEM), vmem],
            out_specs=vmem,
            scratch_shapes=[whole] * (2 * CHUNKS)
            + [
                pltpu.VMEM((slots, CHUNKS, 2, TILE, width), jnp.bfloat16),
                pltpu.VMEM((slots, CHUNKS, 2, TILE, width), jnp.bfloat16),
                pltpu.VMEM((lists, 8, 128), jnp.int32),
                pltpu.SMEM((lists, 8, 128), jnp.int32),
                pltpu.VMEM((heads, rows, HD), jnp.float32),
                pltpu.VMEM((heads, rows, HD), jnp.float32),
                pltpu.VMEM((heads, rows, HD), jnp.float32),
                dma((2, CHUNKS, 2)),
                dma((2, CHUNKS, 2)),
                dma((slots, CHUNKS)),
                dma((slots, CHUNKS)),
                dma((lists,)),
                dma((lists,)),
                dma((lists,)),
            ],
            compiler_params=pltpu.CompilerParams(
                collective_id=0, has_side_effects=True, vmem_limit_bytes=60 << 20
            ),
        )(
            queries,
            key_heads.reshape(tiles, TILE, channels),
            value_heads.reshape(tiles, TILE, channels),
            tile_lists,
            padded,
        )

    in_specs = (
        P(("groups", "frame"), None),
        P(("groups", "frame"), None),
        P(("groups", "frame"), None),
        P("frame", None),
    )
    return jax.shard_map(
        body, mesh=mesh, in_specs=in_specs, out_specs=P(("groups", "frame"), None), check_vma=False
    )
```

profile of v0, /device:TPU:19, one launch (start us, length us, event | category | flops | bytes accessed | tf_op | source)
XLA Modules:
  0.0 71.4 jit_solution(7408250823392013423)
XLA Ops:
  0.0 0.0 copy-start
  0.0 0.7 copy-done
  0.7 0.6 pad.4.refs_4_
  1.3 68.0 %shard_map.46 = bf16[256,1536]{1,0:T(8,128)(2,1)} custom-call(bf16[256,1536]{1,0:T(8,128)(2,1)} %refs_0_.1, bf16[2,128,1536]{2,1,0:T(8,128)(2,1)} %bitcast.2, bf16[2,128,1536]{2,1,0:T(8,128)(2,1)} %bitcast.3, s32[1,8]{1,0:T(1,128)} %refs_3_.1, s32[8,128]{1,0:T(8,128)} %pad.4.refs_4_), custom_call_target="tpu_custom_call" | custom-call | tf_op jit(solution)/shard_map/pallas_call | solution.py:279
  69.3 2.1 %copy.6 = bf16[256,1536]{1,0:T(8,128)(2,1)} copy(bf16[256,1536]{1,0:T(8,128)(2,1)} %shard_map.46) | data formatting | bytes 1572864
Async XLA Ops:
  0.0 0.7 copy-start
where the time goes:
time: 71.6 us; the launch traced here: 71.4 us
  Pallas kernels  68 us (95%)
  local copies, waits for them, and re-layouts  3.31 us (5%)
    pallas_call x1, Pallas kernels, body(): pl.pallas_call(functools.partial(kernel, n, levels, heads), out_shape=jax...  68 us
    unnamed x3, local copies, waits for them, and re-layouts  2.72 us

commit v1 on v0

--- a/solution.py
+++ b/solution.py
@@ -10,7 +10,7 @@
 
 HD = 128
 TILE = 128
-CHUNKS = 2
+CHUNKS = 6
 MESH = pl.DeviceIdType.MESH
 
 CORE, ACROSS, ACROSS_RELAYED, MIRROR, BELOW8, ABOVE8 = range(6)

time: 71.6 us -> 67.5 us (0.943)
  Pallas kernels: 68 us -> 64 us
    pallas_call x1, Pallas kernels: 68 us -> 64 us  [body(): pl.pallas_call(functools.partial(kernel, n, levels, heads), out_shape=jax...]
where the time goes in v1:
time: 67.5 us; the launch traced here: 67.3 us
  Pallas kernels  64 us (95%)
  local copies, waits for them, and re-layouts  3.31 us (5%)
    pallas_call x1, Pallas kernels, body(): pl.pallas_call(functools.partial(kernel, n, levels, heads), out_shape=jax...  64 us
    unnamed x3, local copies, waits for them, and re-layouts  2.72 us

profile of v1, /device:TPU:19, one launch (start us, length us, event | category | flops | bytes accessed | tf_op | source)
XLA Modules:
  0.0 67.3 jit_solution(9356711272102041166)
XLA Ops:
  0.0 0.0 copy-start
  0.0 0.7 copy-done
  0.7 0.6 pad.4.refs_4_
  1.3 64.0 %shard_map.46 = bf16[256,1536]{1,0:T(8,128)(2,1)} custom-call(bf16[256,1536]{1,0:T(8,128)(2,1)} %refs_0_.1, bf16[2,128,1536]{2,1,0:T(8,128)(2,1)} %bitcast.2, bf16[2,128,1536]{2,1,0:T(8,128)(2,1)} %bitcast.3, s32[1,8]{1,0:T(1,128)} %refs_3_.1, s32[8,128]{1,0:T(8,128)} %pad.4.refs_4_), custom_call_target="tpu_custom_call" | custom-call | tf_op jit(solution)/shard_map/pallas_call | solution.py:279
  65.2 2.1 %copy.6 = bf16[256,1536]{1,0:T(8,128)(2,1)} copy(bf16[256,1536]{1,0:T(8,128)(2,1)} %shard_map.46) | data formatting | bytes 1572864
Async XLA Ops:
  0.0 0.7 copy-start
